TPU v7x, 32 devices: a whole 2x2x4 slice. The times are simulated.
32 devices in a mesh: req: 8 (over y, x, core), tp: 4 (over z).
Axes of the slice: x: 2, y: 2, z: 4, core: 2. Of those that a mesh axis runs over, the one named last changes fastest.
Arguments:
- new_query: bfloat16 [1024, 2560], P('req', 'tp'), may hold values from -64 to 64
- new_keyval: bfloat16 [1024, 1280], P('req', 'tp'), may hold values from -24 to 24
- residual_in: bfloat16 [1024, 2560], P('req'), may hold values from -64 to 64
- leaf_cache: bfloat16 [128, 32, 1280], P('req', None, 'tp'), may hold values from -6 to 6
- leaf_length: int32 [128], P('req'), may hold values from 1 to 32
- new_counts: int32 [8, 16], P('req'), may hold values from 1 to 16, as said below
- request_mid: int32 [128], P('req'), may hold values from 0 to 5
- mid_root: int32 [6], replicated, may hold values from 0 to 1, as said below
- node_length: int32 [8], replicated, may hold values from 1 to 1744, as said below
- prefix_pool: bfloat16 [256, 16, 1280], P('req', None, 'tp'), may hold values from -6 to 6
- page_node: int32 [256], P('req'), may hold values from -1 to 7, as said below
- page_rank: int32 [256], P('req'), may hold values from 0 to 108, as said below
- out_weight: bfloat16 [2560, 2560], P('tp'), may hold values from -0.125 to 0.125
- norm_gain: bfloat16 [2560], replicated, may hold values from 0.5 to 1.5
- gate_weight: bfloat16 [2560, 3584], P(None, 'tp'), may hold values from -0.125 to 0.125
- up_weight: bfloat16 [2560, 3584], P(None, 'tp'), may hold values from -0.125 to 0.125
- down_weight: bfloat16 [3584, 2560], P('tp'), may hold values from -0.09375 to 0.09375
- next_gain: bfloat16 [2560], replicated, may hold values from 0.5 to 1.5
- query_weight: bfloat16 [2560, 2560], P(None, 'tp'), may hold values from -0.125 to 0.125
- keyval_weight: bfloat16 [2560, 1280], P(None, 'tp'), may hold values from -0.125 to 0.125
Outputs:
- attention: bfloat16 [1024, 2560], P('req', 'tp')
- residual_out: bfloat16 [1024, 2560], P(('req', 'tp'))
- next_query: bfloat16 [1024, 2560], P('req', 'tp')
- next_keyval: bfloat16 [1024, 1280], P('req', 'tp')
Inputs may be any that keep to these rules, and one draw needn't show every extreme that they name: `new_counts`: each row sums to 128 and holds one request of exactly 16 new tokens. `mid_root`: each root is the parent of 3 mid-level nodes. `node_length`: A node of k pages has more than 16 * (k - 1) and at most 16 * k prefix tokens; a node with the most pages has exactly 16 * k. `page_node`: every node owns one page or more; 32 pages are free (-1). `page_rank`: the k pages of a node carry the ranks 0 to k - 1, each once; free pages carry 0.
All inputs are finite; a program needn't handle non-finite values.
Results may differ from a plain program's by a relative error of at most 0.015.
Values may be sent and summed in bfloat16 or wider, within the bound.
No kernel may reach another device: no remote copies, remote signals or barrier semaphores. Data moves between devices by JAX's collectives and lax.ppermute only.
A program may use at most 128 MiB of HBM per device.

v0:
```python
import math
import jax
import jax.numpy as jnp
from jax import lax
from jax.sharding import PartitionSpec as P

HD = 80
MAXNEW = 16
ROOTS = 2
MIDS = 6
NODES = 8
MASKED = -1e30
EPSILON = 1e-05


def rms_scale(values_in, gain):
    values = values_in.astype(jnp.float32)
    scale = lax.rsqrt(jnp.mean(values * values, axis=-1, keepdims=True) + EPSILON)
    return (values * scale * gain.astype(jnp.float32)).astype(jnp.bfloat16)


def combine(first, second):
    top_first, total_first, sum_first = first
    top_second, total_second, sum_second = second
    top = jnp.maximum(top_first, top_second)
    factor_first = jnp.exp(top_first - top)
    factor_second = jnp.exp(top_second - top)
    total = total_first * factor_first + total_second * factor_second
    weighted = sum_first * factor_first[..., None] + sum_second * factor_second[..., None]
    return (top, total, weighted)


def attend(queries, keys, values, visible):
    scores = jnp.einsum("nkgd,mkd->nkgm", queries, keys, preferred_element_type=jnp.float32) * (
        1.0 / math.sqrt(HD)
    )
    shown = visible[:, None, None, :]
    scores = jnp.where(shown, scores, MASKED)
    top = jnp.max(scores, axis=-1)
    raised = jnp.where(shown, jnp.exp(scores - top[..., None]), 0.0)
    total = jnp.sum(raised, axis=-1)
    weighted = jnp.einsum(
        "nkgm,mkd->nkgd", raised.astype(jnp.bfloat16), values, preferred_element_type=jnp.float32
    )
    return (top, total, weighted)


def pool_split(pages_in, node_of_page, rank_of_page):
    page_count = pages_in.shape[0]
    page_size = pages_in.shape[1]
    flat = pages_in.reshape(page_count * page_size, pages_in.shape[2] // (2 * HD), 2, HD)
    key_node = jnp.repeat(node_of_page, page_size, total_repeat_length=page_count * page_size)
    key_place = (
        rank_of_page[:, None] * page_size + jnp.arange(page_size, dtype=jnp.int32)[None, :]
    ).reshape(page_count * page_size)
    return (flat[:, :, 0], flat[:, :, 1], key_node, key_place)


def shared_visible(token_info, key_node, key_place):
    root_hit = (key_node[None, :] == token_info[:, 0:1]) & (key_place[None, :] < token_info[:, 2:3])
    mid_hit = (key_node[None, :] == token_info[:, 1:2]) & (key_place[None, :] < token_info[:, 3:4])
    return root_hit | mid_hit


def token_tables(counts, request_mid, mid_root, node_length, row_count):
    requests = counts.shape[0]
    starts = jnp.cumsum(counts) - counts
    index = jnp.arange(row_count, dtype=jnp.int32)
    owner = jnp.sum((index[:, None] >= starts[None, :]).astype(jnp.int32), axis=1) - 1
    pick = (owner[:, None] == jnp.arange(requests, dtype=jnp.int32)[None, :]).astype(jnp.int32)
    offset = index - jnp.sum(pick * starts[None, :], axis=1)
    token_mid = jnp.sum(pick * request_mid[None, :], axis=1)
    mid_pick = (token_mid[:, None] == jnp.arange(MIDS, dtype=jnp.int32)[None, :]).astype(jnp.int32)
    token_root = jnp.sum(mid_pick * mid_root[None, :], axis=1)
    mid_node = token_mid + ROOTS
    node_ids = jnp.arange(NODES, dtype=jnp.int32)
    root_len = jnp.sum(
        (token_root[:, None] == node_ids[None, :]).astype(jnp.int32) * node_length[None, :], axis=1
    )
    mid_len = jnp.sum(
        (mid_node[:, None] == node_ids[None, :]).astype(jnp.int32) * node_length[None, :], axis=1
    )
    token_info = jnp.stack([token_root, mid_node, root_len, mid_len], axis=1)
    return (starts, owner, offset, token_info)


def local_part(
    new_query, new_keyval, leaf_cache, leaf_length, counts, starts, owner, offset, kv_local, group
):
    requests = counts.shape[0]
    leaf_slots = leaf_cache.shape[1]
    slot = jnp.arange(MAXNEW, dtype=jnp.int32)
    row_index = jnp.clip(starts[:, None] + slot[None, :], 0, new_query.shape[0] - 1)
    pad_query = new_query[row_index].reshape(requests, MAXNEW, kv_local, group, HD)
    pad_keyval = new_keyval[row_index]
    joined = jnp.concatenate([leaf_cache, pad_keyval], axis=1).reshape(
        requests, leaf_slots + MAXNEW, kv_local, 2, HD
    )
    leaf_ok = jnp.broadcast_to(
        jnp.arange(leaf_slots, dtype=jnp.int32)[None, None, :] < leaf_length[:, None, None],
        (requests, MAXNEW, leaf_slots),
    )
    causal = jnp.broadcast_to(
        slot[None, None, :] <= slot[None, :, None], (requests, MAXNEW, MAXNEW)
    )
    visible = jnp.concatenate([leaf_ok, causal], axis=2)
    part = jax.vmap(attend)(pad_query, joined[:, :, :, 0], joined[:, :, :, 1], visible)
    flat = owner * MAXNEW + offset
    return tuple((item.reshape((requests * MAXNEW,) + item.shape[2:])[flat] for item in part))


def visit_owners(new_query, token_info, prefix_pool, page_node, page_rank, kv_local, group):
    all_query, all_info = (
        lax.all_gather(new_query, "req", axis=0, tiled=True),
        lax.all_gather(token_info, "req", axis=0, tiled=True),
    )
    total_rows = all_query.shape[0]
    block = math.gcd(total_rows, 512)
    keys, values, key_node, key_place = pool_split(prefix_pool, page_node, page_rank)

    def owner_block(items):
        query_block, info_block = items
        heads = query_block.reshape(block, kv_local, group, HD)
        return attend(heads, keys, values, shared_visible(info_block, key_node, key_place))

    part = lax.map(
        owner_block,
        (
            all_query.reshape(total_rows // block, block, all_query.shape[1]),
            all_info.reshape(total_rows // block, block, 4),
        ),
    )
    holders = lax.axis_size("req")
    row_count = total_rows // holders
    part_top, part_total, part_sum = tuple(
        (item.reshape((holders, row_count) + item.shape[2:]) for item in part)
    )
    tops, totals, sums = (
        lax.all_to_all(part_top, "req", split_axis=0, concat_axis=0, tiled=True),
        lax.all_to_all(part_total, "req", split_axis=0, concat_axis=0, tiled=True),
        lax.all_to_all(part_sum, "req", split_axis=0, concat_axis=0, tiled=True),
    )
    top = jnp.max(tops, axis=0)
    factor = jnp.exp(tops - top[None])
    return (top, jnp.sum(totals * factor, axis=0), jnp.sum(sums * factor[..., None], axis=0))


def per_device(
    new_query,
    new_keyval,
    residual_in,
    leaf_cache,
    leaf_length,
    new_counts,
    request_mid,
    mid_root,
    node_length,
    prefix_pool,
    page_node,
    page_rank,
    out_weight,
    norm_gain,
    gate_weight,
    up_weight,
    down_weight,
    next_gain,
    query_weight,
    keyval_weight,
):
    row_count = new_query.shape[0]
    query_width = new_query.shape[1]
    keyval_width = new_keyval.shape[1]
    kv_local = keyval_width // (2 * HD)
    group = query_width // (kv_local * HD)
    counts = new_counts[0]
    starts, owner, offset, token_info = token_tables(
        counts, request_mid, mid_root, node_length, row_count
    )
    shared = visit_owners(new_query, token_info, prefix_pool, page_node, page_rank, kv_local, group)
    local = local_part(
        new_query,
        new_keyval,
        leaf_cache,
        leaf_length,
        counts,
        starts,
        owner,
        offset,
        kv_local,
        group,
    )
    top, total, weighted = combine(shared, local)
    attention = (weighted / total[..., None]).reshape(row_count, query_width).astype(jnp.bfloat16)
    share = row_count // lax.axis_size("tp")
    mine = lax.axis_index("tp") * share
    attn_proj = lax.psum(jnp.dot(attention, out_weight, preferred_element_type=jnp.float32), "tp")
    mixed = (residual_in.astype(jnp.float32) + attn_proj).astype(jnp.bfloat16)
    normed = rms_scale(mixed, norm_gain)
    gate = jnp.dot(normed, gate_weight, preferred_element_type=jnp.float32)
    upward = jnp.dot(normed, up_weight, preferred_element_type=jnp.float32)
    hidden = (jax.nn.silu(gate) * upward).astype(jnp.bfloat16)
    mlp_proj = lax.psum(jnp.dot(hidden, down_weight, preferred_element_type=jnp.float32), "tp")
    layer_rows = (mixed.astype(jnp.float32) + mlp_proj).astype(jnp.bfloat16)
    residual_out = lax.dynamic_slice_in_dim(layer_rows, mine, share, 0)
    final = rms_scale(layer_rows, next_gain)
    next_query = jnp.dot(final, query_weight, preferred_element_type=jnp.float32).astype(
        jnp.bfloat16
    )
    next_keyval = jnp.dot(final, keyval_weight, preferred_element_type=jnp.float32).astype(
        jnp.bfloat16
    )
    return (attention, residual_out, next_query, next_keyval)


def solution(mesh):
    in_specs = (
        P("req", "tp"),
        P("req", "tp"),
        P("req", None),
        P("req", None, "tp"),
        P("req"),
        P("req", None),
        P("req"),
        P(),
        P(),
        P("req", None, "tp"),
        P("req"),
        P("req"),
        P("tp", None),
        P(),
        P(None, "tp"),
        P(None, "tp"),
        P("tp", None),
        P(),
        P(None, "tp"),
        P(None, "tp"),
    )
    out_specs = (P("req", "tp"), P(("req", "tp"), None), P("req", "tp"), P("req", "tp"))
    return jax.shard_map(
        per_device, mesh=mesh, in_specs=in_specs, out_specs=out_specs, check_vma=False
    )
```

profile of v0, /device:TPU:0, one launch (start us, length us, event | category | flops | bytes accessed | tf_op | source)
XLA Modules:
  0.0 375.2 jit_solution(16658785647169500201)
XLA Ops:
  10.4 2.1 reshape.441
  12.5 3.1 fusion.62
  16.4 1.8 copy.129
  18.2 1.8 copy.128
  20.8 11.4 %all_gather.6 = s32[1024,4]{0,1:T(4,128)} all-gather(s32[128,4]{0,1:T(4,128)S(1)} %pad_add_fusion.1), channel_id=1, replica_groups=mesh['req'=8,'tp'=4] {'req'}, dimensions={0}, use_global_device_ids=true | all-gather | bytes 18432 | tf_op jit(solution)/shard_map/all_gather | solution.py:115
  33.8 4.2 %compare_select_fusion.2 = (s32[512,1]{0,1:T(1,128)S(1)}, s32[512,1]{0,1:T(1,128)S(1)}) fusion(s32[]{:T(128)} %bitcast.29, s32[]{:T(128)} %bitcast.30, s32[]{:T(128)} %bitcast.31, s32[]{:T(128)} %bitcast.32, s32[]{:T(128)} %bitcast.33, s32[]{:T(128)} %bitcast.35, s32[]{:T(128)} %bitcast.34, s32[512,1]{0,1:T(1,128)S(1)} %bitcast.213, s32[512,1]{0,1:T(1,128)S(1)} %bitcast.212), kind=kLoop, calls=%fused_computation.105 | loop fusion | flops 7168 | bytes 8220 | tf_op jit(solution)/shard_map/jit(_take)/gather | solution.py:52
  38.6 16.0 %select_select_fusion = s32[512]{0:T(512)} fusion(pred[512]{0:T(512)(128)(4,1)S(1)} %get-tuple-element.200, pred[512]{0:T(512)(128)(4,1)S(1)} %get-tuple-element.199, pred[512]{0:T(512)(128)(4,1)S(1)} %get-tuple-element.198, pred[512]{0:T(512)(128)(4,1)S(1)} %get-tuple-element.197, pred[512]{0:T(512)(128)(4,1)S(1)} %get-tuple-element.196, ...), kind=kLoop, calls=%fused_computation.129 | loop fusion | flops 17408 | bytes 19060 | tf_op jit(solution)/shard_map/jit(_take)/select_n | solution.py:52
  54.6 100.4 %while.16 = (s32[]{:T(128)}, f32[2,512,2,4]{1,0,3,2:T(2,128)}, f32[2,512,2,4]{1,0,3,2:T(2,128)}, f32[2,512,2,4,80]{1,0,4,3,2:T(2,128)}, s32[512]{0:T(512)}, /*in...) while((s32[]{:T(128)}, f32[2,512,2,4]{1,0,3,2:T(2,128)}, ...), condition=%wide.region_9.10_spmd.clone, body=%wide.region_6.0_spmd.clone.sunk | while | flops 700178944 | bytes 71092600 | solution.py:126
  57.8 2.0 constant_dynamic-slice_fusion.3
  59.8 2.2 copy.193
  62.0 5.8 %bitcast_reduce_fusion.2 = (f32[512,2,4]{0,2,1:T(4,128)S(1)}, f32[2,512,4,512]{1,3,2,0:T(8,128)}) fusion(pred[512,512]{0,1:T(8,128)(4,1)S(1)} %and_or_fusion.2, bf16[512,2,4,80]{0,3,2,1:T(8,128)(2,1)} %bitcast.188, bf16[512,2,80]{0,2,1:T(8,128)(2,1)} %get-tuple-element.391), kind=kOutput, calls=%fused_computation.7.clone.1 | convolution fusion | flops 341831680 | bytes 9486336 | tf_op jit(solution)/shard_map/while/body/eval_jaxpr/nkgd,mkd->nkgm/dot_general | solution.py:34
  69.9 4.6 %fusion.85 = f32[512,2,4]{0,2,1:T(4,128)S(1)} fusion(f32[2,512,4,512]{1,3,2,0:T(8,128)} %get-tuple-element.359, f32[512,2,4]{0,2,1:T(4,128)S(1)} %get-tuple-element.358, pred[512,512]{0,1:T(8,128)(4,1)S(1)} %and_or_fusion.2), kind=kLoop, calls=%fused_computation.12.clone.1 | loop fusion | flops 10481664 | bytes 8683520 | tf_op jit(solution)/shard_map/while/body/eval_jaxpr/reduce_sum | solution.py:41
  75.8 2.3 fusion.86
  78.1 2.4 copy.196
  80.6 24.2 %dynamic_update_slice.19 = f32[2,512,2,4,80]{1,0,4,3,2:T(2,128)} dynamic-update-slice(f32[2,512,2,4,80]{1,0,4,3,2:T(2,128)} %get-tuple-element.375, f32[1,512,2,4,80]{1,0,4,3,2:T(1,128)} %copy.196, s32[]{:T(128)S(6)} %copy.204, s32[]{:T(128)} %constant.138.clone.1..sunk, s32[]{:T(128)} %constant.138.clone.1..sunk, s32[]{:T(128)} %constant.138.clone.1..sunk, s32[]{:T(128)} %constant.138.clone.1..sunk) | dynamic-update-slice | bytes 2621444 | tf_op jit(solution)/shard_map/while/body/jit(dynamic_update_index_in_dim)/dynamic_update_slice | solution.py:126
  108.1 2.0 constant_dynamic-slice_fusion.3
  110.0 2.2 copy.193
  112.2 5.8 %bitcast_reduce_fusion.2 = (f32[512,2,4]{0,2,1:T(4,128)S(1)}, f32[2,512,4,512]{1,3,2,0:T(8,128)}) fusion(pred[512,512]{0,1:T(8,128)(4,1)S(1)} %and_or_fusion.2, bf16[512,2,4,80]{0,3,2,1:T(8,128)(2,1)} %bitcast.188, bf16[512,2,80]{0,2,1:T(8,128)(2,1)} %get-tuple-element.391), kind=kOutput, calls=%fused_computation.7.clone.1 | convolution fusion | flops 341831680 | bytes 9486336 | tf_op jit(solution)/shard_map/while/body/eval_jaxpr/nkgd,mkd->nkgm/dot_general | solution.py:34
  120.1 4.6 %fusion.85 = f32[512,2,4]{0,2,1:T(4,128)S(1)} fusion(f32[2,512,4,512]{1,3,2,0:T(8,128)} %get-tuple-element.359, f32[512,2,4]{0,2,1:T(4,128)S(1)} %get-tuple-element.358, pred[512,512]{0,1:T(8,128)(4,1)S(1)} %and_or_fusion.2), kind=kLoop, calls=%fused_computation.12.clone.1 | loop fusion | flops 10481664 | bytes 8683520 | tf_op jit(solution)/shard_map/while/body/eval_jaxpr/reduce_sum | solution.py:41
  126.0 2.3 fusion.86
  128.3 2.4 copy.196
  130.8 24.2 %dynamic_update_slice.19 = f32[2,512,2,4,80]{1,0,4,3,2:T(2,128)} dynamic-update-slice(f32[2,512,2,4,80]{1,0,4,3,2:T(2,128)} %get-tuple-element.375, f32[1,512,2,4,80]{1,0,4,3,2:T(1,128)} %copy.196, s32[]{:T(128)S(6)} %copy.204, s32[]{:T(128)} %constant.138.clone.1..sunk, s32[]{:T(128)} %constant.138.clone.1..sunk, s32[]{:T(128)} %constant.138.clone.1..sunk, s32[]{:T(128)} %constant.138.clone.1..sunk) | dynamic-update-slice | bytes 2621444 | tf_op jit(solution)/shard_map/while/body/jit(dynamic_update_index_in_dim)/dynamic_update_slice | solution.py:126
  156.5 4.0 %all-to-all-start.1 = ((f32[8,128,2,4]{1,3,2,0:T(4,128)}), f32[8,128,2,4]{1,3,2,0:T(4,128)}, u32[]{:S(2)}, u32[]{:S(2)}) async-start(f32[8,128,2,4]{1,3,2,0:T(4,128)} %copy.135), calls=%async_computation.1 | async-start | bytes 65536 | tf_op jit(solution)/shard_map/all_to_all | solution.py:139
  162.1 1.8 gather_fusion
  165.4 4.1 %all-to-all-start.2 = ((f32[8,128,2,4]{1,3,2,0:T(4,128)}), f32[8,128,2,4]{1,3,2,0:T(4,128)S(1)}, u32[]{:S(2)}, u32[]{:S(2)}) async-start(f32[8,128,2,4]{1,3,2,0:T(4,128)} %copy.150), calls=%async_computation.2 | async-start | bytes 65536 | tf_op jit(solution)/shard_map/all_to_all | solution.py:140
  169.5 2.0 pad_maximum_fusion
  171.4 1.9 gather_fusion.1
  173.4 2.3 reshape.447
  175.7 3.7 reshape.446
  179.4 4.7 %reshape.442 = f32[8,128,2,4,80]{1,0,4,3,2:T(8,128)} reshape(f32[2,512,2,4,80]{1,0,4,3,2:T(2,128)} %get-tuple-element.70) | data formatting | bytes 5242880 | tf_op jit(solution)/shard_map/reshape | solution.py:136
  184.1 3.7 copy.133
  188.5 4.4 %all-to-all-start = ((f32[8,128,2,4,80]{1,4,3,2,0:T(8,128)}), f32[8,128,2,4,80]{1,4,3,2,0:T(8,128)}, u32[]{:S(2)}, u32[]{:S(2)}) async-start(f32[8,128,2,4,80]{1,4,3,2,0:T(8,128)} %copy.133), calls=%async_computation | async-start | bytes 5242880 | tf_op jit(solution)/shard_map/all_to_all | solution.py:141
  193.2 3.7 fusion.61
  199.3 1.9 convolution_bitcast_fusion
  203.0 2.9 gather_fusion.3
  205.9 2.0 copy.148
  207.9 1.7 gather_fusion.2
  209.7 2.5 fusion.30
  217.3 7.9 %all-to-all-done = f32[8,128,2,4,80]{1,4,3,2,0:T(8,128)} async-done(((f32[8,128,2,4,80]{1,4,3,2,0:T(8,128)}), f32[8,128,2,4,80]{1,4,3,2,0:T(8,128)}, u32[]{:S(2)}, u32[]{:S(2)}) %all-to-all-start) | async-done | bytes 2621472 | tf_op jit(solution)/shard_map/all_to_all | solution.py:141
  225.2 2.1 multiply_reduce_fusion
  227.4 1.8 fusion.66
  229.5 59.2 %all-reduce.3.cloned.1.call-done = f32[128,2560]{1,0:T(8,128)} async-done(((f32[128,2560]{1,0:T(8,128)}), f32[128,2560]{1,0:T(8,128)}) %all-reduce.3.cloned.1.call-update) | async-done | bytes 1310736 | tf_op jit(solution)/shard_map/psum | solution.py:196
  288.7 1.8 fusion.24
  291.3 4.0 %fusion.45 = f32[128,896]{1,0:T(8,128)} fusion(bf16[2560,896]{1,0:T(8,128)(2,1)} %param.38, bf16[128,2560]{1,0:T(8,128)(2,1)S(1)} %get-tuple-element.228, f32[2560]{0:T(1024)S(1)} %convert_element_type.63, f32[128]{0:T(128)S(1)} %add_rsqrt_fusion.1), kind=kOutput, calls=%fused_computation.67 | convolution fusion | flops 588513280 | bytes 5712384 | tf_op jit(solution)/shard_map/dot_general | solution.py:199
  295.3 6.7 %fusion.29 = f32[128,2560]{1,0:T(8,128)} fusion(bf16[896,2560]{1,0:T(8,128)(2,1)} %param.40, bf16[2560,896]{1,0:T(8,128)(2,1)} %param.39, f32[128,896]{1,0:T(8,128)} %fusion.45, bf16[128,2560]{1,0:T(8,128)(2,1)} %copy-done.3, f32[2560]{0:T(1024)S(1)} %convert_element_type.63, f32[128]{0:T(128)S(1)} %add_rsqrt_fusion.1), kind=kOutput, calls=%fused_computation.50 | convolution fusion | flops 1176403968 | bytes 11610624 | tf_op jit(solution)/shard_map/dot_general | solution.py:202
  302.9 59.0 %all-reduce.5.cloned.1.call-done = f32[128,2560]{1,0:T(8,128)} async-done(((f32[128,2560]{1,0:T(8,128)}), f32[128,2560]{1,0:T(8,128)}) %all-reduce.5.cloned.1.call-update) | async-done | bytes 1310736 | tf_op jit(solution)/shard_map/psum | solution.py:202
  361.9 1.9 fusion.21
  363.8 2.7 convolution_convert_fusion.1
  (136 shorter events, 38.8 us)
Async XLA Ops:
  7.2 220.2 %copy-start = (bf16[640,2560]{1,0:T(8,128)(2,1)S(1)}, bf16[640,2560]{1,0:T(8,128)(2,1)}, u32[]{:S(2)}) copy-start(bf16[640,2560]{1,0:T(8,128)(2,1)} %param.36) | copy-start | bytes 9830404
  7.2 26.5 %copy-start.11 = (s32[4,128]{1,0:T(4,128)S(1)}, s32[4,128]{1,0:T(4,128)}, u32[]{:S(2)}) copy-start(s32[4,128]{1,0:T(4,128)} %constant.143.clone.1) | copy-start | bytes 6148
  7.2 12.8 %copy-start.14 = (s32[16]{0:T(128)S(1)}, s32[16]{0:T(128)}, u32[]{:S(2)}) copy-start(s32[16]{0:T(128)} %param.30) | copy-start | bytes 196
  7.2 13.4 %copy-start.19 = (s32[6]{0:T(128)S(1)}, s32[6]{0:T(128)}, u32[]{:S(2)}) copy-start(s32[6]{0:T(128)} %param.31) | copy-start | bytes 76
  7.2 13.5 %copy-start.15 = (s32[8]{0:T(128)S(1)}, s32[8]{0:T(128)}, u32[]{:S(2)}) copy-start(s32[8]{0:T(128)} %param.32) | copy-start | bytes 100
  7.2 25.0 %copy-start.5 = (s32[32]{0:T(128)S(1)}, s32[32]{0:T(128)}, u32[]{:S(2)}) copy-start(s32[32]{0:T(128)} %param.34) | copy-start | bytes 388
  7.2 30.9 %copy-start.20 = (s32[32]{0:T(128)S(1)}, s32[32]{0:T(128)}, u32[]{:S(2)}) copy-start(s32[32]{0:T(128)} %param.35) | copy-start | bytes 388
  7.2 47.4 %all-gather.2.cloned.1.call-start = ((), (), s32[]{:S(2)}) async-start(), calls=%async_computation.3 | async-start | bytes 1474560 | tf_op jit(solution)/shard_map/all_gather | solution.py:114
  15.7 5.0 %copy-start.21 = (s32[128]{0:T(128)}, s32[128]{0:T(128)S(1)}, u32[]{:S(2)}) copy-start(s32[128]{0:T(128)S(1)} %convert_reduce_fusion) | copy-start | bytes 1540
  69.9 5.8 %copy-start.1 = (f32[2,512,4,512]{1,3,2,0:T(8,128)S(1)}, f32[2,512,4,512]{1,3,2,0:T(8,128)}, u32[]{:S(2)}) copy-start(f32[2,512,4,512]{1,3,2,0:T(8,128)} %get-tuple-element.359) | copy-start | bytes 25165828 | tf_op jit(solution)/shard_map/while
  69.9 5.8 %copy-start.7 = (bf16[512,2,80]{0,2,1:T(8,128)(2,1)S(1)}, bf16[512,2,80]{0,2,1:T(8,128)(2,1)}, u32[]{:S(2)}) copy-start(bf16[512,2,80]{0,2,1:T(8,128)(2,1)} %get-tuple-element.392) | copy-start | bytes 491524 | tf_op jit(solution)/shard_map/while
  78.1 2.4 copy-start.9
  80.6 24.2 %copy-start.10 = (f32[2,512,2,4]{1,0,3,2:T(2,128)}, f32[2,512,2,4]{1,0,3,2:T(2,128)S(1)}, u32[]{:S(2)}) copy-start(f32[2,512,2,4]{1,0,3,2:T(2,128)S(1)} %dynamic_update_slice.18) | copy-start | bytes 98308 | tf_op jit(solution)/shard_map/while
  120.1 5.8 %copy-start.1 = (f32[2,512,4,512]{1,3,2,0:T(8,128)S(1)}, f32[2,512,4,512]{1,3,2,0:T(8,128)}, u32[]{:S(2)}) copy-start(f32[2,512,4,512]{1,3,2,0:T(8,128)} %get-tuple-element.359) | copy-start | bytes 25165828 | tf_op jit(solution)/shard_map/while
  120.1 5.8 %copy-start.7 = (bf16[512,2,80]{0,2,1:T(8,128)(2,1)S(1)}, bf16[512,2,80]{0,2,1:T(8,128)(2,1)}, u32[]{:S(2)}) copy-start(bf16[512,2,80]{0,2,1:T(8,128)(2,1)} %get-tuple-element.392) | copy-start | bytes 491524 | tf_op jit(solution)/shard_map/while
  128.3 2.4 copy-start.9
  130.8 24.2 %copy-start.10 = (f32[2,512,2,4]{1,0,3,2:T(2,128)}, f32[2,512,2,4]{1,0,3,2:T(2,128)S(1)}, u32[]{:S(2)}) copy-start(f32[2,512,2,4]{1,0,3,2:T(2,128)S(1)} %dynamic_update_slice.18) | copy-start | bytes 98308 | tf_op jit(solution)/shard_map/while
  155.1 16.4 %copy-start.2 = (bf16[128,640]{1,0:T(8,128)(2,1)S(1)}, bf16[128,640]{1,0:T(8,128)(2,1)}, u32[]{:S(2)}) copy-start(bf16[128,640]{1,0:T(8,128)(2,1)} %param.24) | copy-start | bytes 491524
  156.5 8.8 %all-to-all-start.1 = ((f32[8,128,2,4]{1,3,2,0:T(4,128)}), f32[8,128,2,4]{1,3,2,0:T(4,128)}, u32[]{:S(2)}, u32[]{:S(2)}) async-start(f32[8,128,2,4]{1,3,2,0:T(4,128)} %copy.135), calls=%async_computation.1 | async-start | bytes 65536 | tf_op jit(solution)/shard_map/all_to_all | solution.py:139
  165.4 22.5 %all-to-all-start.2 = ((f32[8,128,2,4]{1,3,2,0:T(4,128)}), f32[8,128,2,4]{1,3,2,0:T(4,128)S(1)}, u32[]{:S(2)}, u32[]{:S(2)}) async-start(f32[8,128,2,4]{1,3,2,0:T(4,128)} %copy.150), calls=%async_computation.2 | async-start | bytes 65536 | tf_op jit(solution)/shard_map/all_to_all | solution.py:140
  187.9 5.1 %copy-start.16 = (s32[16]{0:T(128)S(1)}, s32[16]{0:T(128)}, u32[]{:S(2)}) copy-start(s32[16]{0:T(128)} %param.28) | copy-start | bytes 196
  187.9 0.6 copy-start.8
  188.5 36.7 %all-to-all-start = ((f32[8,128,2,4,80]{1,4,3,2,0:T(8,128)}), f32[8,128,2,4,80]{1,4,3,2,0:T(8,128)}, u32[]{:S(2)}, u32[]{:S(2)}) async-start(f32[8,128,2,4,80]{1,4,3,2,0:T(8,128)} %copy.133), calls=%async_computation | async-start | bytes 5242880 | tf_op jit(solution)/shard_map/all_to_all | solution.py:141
  192.9 95.8 %all-reduce.3.cloned.1.call-start = ((), (), s32[]{:S(2)}) async-start(), calls=%async_computation.4 | async-start | bytes 2621440 | tf_op jit(solution)/shard_map/psum | solution.py:196
  193.0 4.0 %copy-start.6 = (bf16[16,16,2,4,80]{4,3,2,1,0:T(4,128)(2,1)S(1)}, bf16[16,16,2,4,80]{4,3,2,1,0:T(4,128)(2,1)}, u32[]{:S(2)}) copy-start(bf16[16,16,2,4,80]{4,3,2,1,0:T(4,128)(2,1)} %reshape.447) | copy-start | bytes 983044
  201.2 1.8 copy-start.17
  201.2 1.8 copy-start.22
  225.2 2.1 copy-start.4
  227.3 2.1 copy-start.12
  229.2 132.7 %all-reduce.5.cloned.1.call-start = ((), (), s32[]{:S(2)}) async-start(), calls=%async_computation.5 | async-start | bytes 2621440 | tf_op jit(solution)/shard_map/psum | solution.py:202
  290.5 0.9 copy-start.3
  295.3 6.8 %copy-start.13 = (bf16[2560]{0:T(1024)(128)(2,1)S(1)}, bf16[2560]{0:T(1024)(128)(2,1)}, u32[]{:S(2)}) copy-start(bf16[2560]{0:T(1024)(128)(2,1)} %param.41) | copy-start | bytes 15364
  361.9 4.7 %copy-start.18 = (bf16[2560,640]{1,0:T(8,128)(2,1)S(1)}, bf16[2560,640]{1,0:T(8,128)(2,1)}, u32[]{:S(2)}) copy-start(bf16[2560,640]{1,0:T(8,128)(2,1)} %param.42) | copy-start | bytes 9830404
Sparse Core Ops, SparseCore 0:
  10.0 27.2 all-gather.1
  229.3 59.3 all-reduce.2
  302.2 59.6 all-reduce.4
where the time goes:
time: 381 us; the launch traced here: 375 us
  waiting for transfers between devices  127 us (33%)
  local copies, waits for them, and re-layouts  125 us (33%)
  other arithmetic  49 us (13%)
  matrix products  36.3 us (10%)
  between operations  14.1 us (4%)
  starting transfers between devices  12.8 us (3%)
  blocking collectives  11.4 us (3%)
    psum x1, waiting for transfers between devices, per_device(): lax.psum(jnp.dot(attention, out_weight, preferred_element_type=jnp.float3...  59.2 us
    psum x1, waiting for transfers between devices, per_device(): lax.psum(jnp.dot(hidden, down_weight, preferred_element_type=jnp.float32)...  59 us
    dynamic_update_slice x12, local copies, waits for them, and re-layouts, visit_owners(): lax.map(owner_block, (all_query.reshape(total_rows // block, block, all_q...  57.6 us
    select_n x1, other arithmetic, pool_split(): jnp.repeat(node_of_page, page_size, total_repeat_length=page_count * page...  16 us
    dot_general x3, matrix products, attend(): jnp.einsum('nkgd,mkd->nkgm', queries, keys, preferred_element_type=jnp.fl...  13.1 us
    reduce_sum x3, other arithmetic, attend(): total = jnp.sum(raised, axis=-1)  11.8 us
    all_gather x1, blocking collectives, visit_owners(): lax.all_gather(token_info, 'req', axis=0, tiled=True)  11.4 us
    reshape x6, local copies, waits for them, and re-layouts, visit_owners(): item.reshape((holders, row_count) + item.shape[2:])  11.4 us
  transfers between devices with their start and end apart: 6, of which 3 were waited for; matrix products, arithmetic and copies ran while one was open for 22% of the time, Pallas kernels for 0%

commit v1 on v0

--- a/solution.py
+++ b/solution.py
@@ -193,7 +193,12 @@
     attention = (weighted / total[..., None]).reshape(row_count, query_width).astype(jnp.bfloat16)
     share = row_count // lax.axis_size("tp")
     mine = lax.axis_index("tp") * share
-    attn_proj = lax.psum(jnp.dot(attention, out_weight, preferred_element_type=jnp.float32), "tp")
+    attn_proj = jnp.sum(
+        lax.all_gather(
+            jnp.dot(attention, out_weight, preferred_element_type=jnp.float32), axis_name="tp"
+        ),
+        0,
+    )
     mixed = (residual_in.astype(jnp.float32) + attn_proj).astype(jnp.bfloat16)
     normed = rms_scale(mixed, norm_gain)
     gate = jnp.dot(normed, gate_weight, preferred_element_type=jnp.float32)

time: 381 us -> 422 us (1.11)
  waiting for transfers between devices: 127 us -> 164 us
    all_gather x0 -> x1, waiting for transfers between devices: none -> 97.3 us  [per_device(): lax.all_gather(jnp.dot(attention, out_weight, preferred_element_type=jnp....]
    psum x1 -> x0, waiting for transfers between devices: 59.2 us -> none  [per_device(): lax.psum(jnp.dot(attention, out_weight, preferred_element_type=jnp.float3...]
  transfers between devices with their start and end apart: 6 -> 6, of which waited for: 3 -> 3; matrix products, arithmetic and copies ran while one was open for 22% -> 20% of each run, Pallas kernels for 0% -> 0%
where the time goes in v1:
time: 422 us; the launch traced here: 416 us
  waiting for transfers between devices  164 us (39%)
  local copies, waits for them, and re-layouts  125 us (30%)
  other arithmetic  53.1 us (13%)
  matrix products  36.3 us (9%)
  between operations  14.1 us (3%)
  starting transfers between devices  12.8 us (3%)
  blocking collectives  11.4 us (3%)
    all_gather x1, waiting for transfers between devices, per_device(): lax.all_gather(jnp.dot(attention, out_weight, preferred_element_type=jnp....  97.3 us
    psum x1, waiting for transfers between devices, per_device(): lax.psum(jnp.dot(hidden, down_weight, preferred_element_type=jnp.float32)...  57.7 us
    dynamic_update_slice x12, local copies, waits for them, and re-layouts, visit_owners(): lax.map(owner_block, (all_query.reshape(total_rows // block, block, all_q...  57.6 us
    select_n x1, other arithmetic, pool_split(): jnp.repeat(node_of_page, page_size, total_repeat_length=page_count * page...  16 us
    dot_general x3, matrix products, attend(): jnp.einsum('nkgd,mkd->nkgm', queries, keys, preferred_element_type=jnp.fl...  13.1 us
    reduce_sum x3, other arithmetic, attend(): total = jnp.sum(raised, axis=-1)  11.8 us
    all_gather x1, blocking collectives, visit_owners(): lax.all_gather(token_info, 'req', axis=0, tiled=True)  11.4 us
    reshape x6, local copies, waits for them, and re-layouts, visit_owners(): item.reshape((holders, row_count) + item.shape[2:])  11.4 us
  transfers between devices with their start and end apart: 6, of which 3 were waited for; matrix products, arithmetic and copies ran while one was open for 20% of the time, Pallas kernels for 0%

profile of v1, /device:TPU:0, one launch (start us, length us, event | category | flops | bytes accessed | tf_op | source)
XLA Modules:
  0.0 416.1 jit_solution(8402770698400928321)
XLA Ops:
  10.4 2.1 reshape.441
  12.5 3.1 fusion.62
  16.4 1.8 copy.129
  18.2 1.8 copy.128
  20.8 11.4 %all_gather.12 = s32[1024,4]{0,1:T(4,128)} all-gather(s32[128,4]{0,1:T(4,128)S(1)} %pad_add_fusion.1), channel_id=1, replica_groups=mesh['req'=8,'tp'=4] {'req'}, dimensions={0}, use_global_device_ids=true | all-gather | bytes 18432 | tf_op jit(solution)/shard_map/all_gather | solution.py:115
  33.8 4.2 %compare_select_fusion.2 = (s32[512,1]{0,1:T(1,128)S(1)}, s32[512,1]{0,1:T(1,128)S(1)}) fusion(s32[]{:T(128)} %bitcast.29, s32[]{:T(128)} %bitcast.30, s32[]{:T(128)} %bitcast.31, s32[]{:T(128)} %bitcast.32, s32[]{:T(128)} %bitcast.33, s32[]{:T(128)} %bitcast.35, s32[]{:T(128)} %bitcast.34, s32[512,1]{0,1:T(1,128)S(1)} %bitcast.215, s32[512,1]{0,1:T(1,128)S(1)} %bitcast.214), kind=kLoop, calls=%fused_computation.105 | loop fusion | flops 7168 | bytes 8220 | tf_op jit(solution)/shard_map/jit(_take)/gather | solution.py:52
  38.6 16.0 %select_select_fusion = s32[512]{0:T(512)} fusion(pred[512]{0:T(512)(128)(4,1)S(1)} %get-tuple-element.200, pred[512]{0:T(512)(128)(4,1)S(1)} %get-tuple-element.199, pred[512]{0:T(512)(128)(4,1)S(1)} %get-tuple-element.198, pred[512]{0:T(512)(128)(4,1)S(1)} %get-tuple-element.197, pred[512]{0:T(512)(128)(4,1)S(1)} %get-tuple-element.196, ...), kind=kLoop, calls=%fused_computation.129 | loop fusion | flops 17408 | bytes 19060 | tf_op jit(solution)/shard_map/jit(_take)/select_n | solution.py:52
  54.6 100.4 %while.16 = (s32[]{:T(128)}, f32[2,512,2,4]{1,0,3,2:T(2,128)}, f32[2,512,2,4]{1,0,3,2:T(2,128)}, f32[2,512,2,4,80]{1,0,4,3,2:T(2,128)}, s32[512]{0:T(512)}, /*in...) while((s32[]{:T(128)}, f32[2,512,2,4]{1,0,3,2:T(2,128)}, ...), condition=%wide.region_9.10_spmd.clone, body=%wide.region_6.0_spmd.clone.sunk | while | flops 700178944 | bytes 71092600 | solution.py:126
  57.8 2.0 constant_dynamic-slice_fusion.3
  59.8 2.2 copy.194
  62.0 5.8 %bitcast_reduce_fusion.2 = (f32[512,2,4]{0,2,1:T(4,128)S(1)}, f32[2,512,4,512]{1,3,2,0:T(8,128)}) fusion(pred[512,512]{0,1:T(8,128)(4,1)S(1)} %and_or_fusion.2, bf16[512,2,4,80]{0,3,2,1:T(8,128)(2,1)} %bitcast.189, bf16[512,2,80]{0,2,1:T(8,128)(2,1)} %get-tuple-element.391), kind=kOutput, calls=%fused_computation.7.clone.1 | convolution fusion | flops 341831680 | bytes 9486336 | tf_op jit(solution)/shard_map/while/body/eval_jaxpr/nkgd,mkd->nkgm/dot_general | solution.py:34
  69.9 4.6 %fusion.85 = f32[512,2,4]{0,2,1:T(4,128)S(1)} fusion(f32[2,512,4,512]{1,3,2,0:T(8,128)} %get-tuple-element.359, f32[512,2,4]{0,2,1:T(4,128)S(1)} %get-tuple-element.358, pred[512,512]{0,1:T(8,128)(4,1)S(1)} %and_or_fusion.2), kind=kLoop, calls=%fused_computation.12.clone.1 | loop fusion | flops 10481664 | bytes 8683520 | tf_op jit(solution)/shard_map/while/body/eval_jaxpr/reduce_sum | solution.py:41
  75.8 2.3 fusion.86
  78.1 2.4 copy.197
  80.6 24.2 %dynamic_update_slice.19 = f32[2,512,2,4,80]{1,0,4,3,2:T(2,128)} dynamic-update-slice(f32[2,512,2,4,80]{1,0,4,3,2:T(2,128)} %get-tuple-element.375, f32[1,512,2,4,80]{1,0,4,3,2:T(1,128)} %copy.197, s32[]{:T(128)S(6)} %copy.205, s32[]{:T(128)} %constant.138.clone.1..sunk, s32[]{:T(128)} %constant.138.clone.1..sunk, s32[]{:T(128)} %constant.138.clone.1..sunk, s32[]{:T(128)} %constant.138.clone.1..sunk) | dynamic-update-slice | bytes 2621444 | tf_op jit(solution)/shard_map/while/body/jit(dynamic_update_index_in_dim)/dynamic_update_slice | solution.py:126
  108.1 2.0 constant_dynamic-slice_fusion.3
  110.0 2.2 copy.194
  112.2 5.8 %bitcast_reduce_fusion.2 = (f32[512,2,4]{0,2,1:T(4,128)S(1)}, f32[2,512,4,512]{1,3,2,0:T(8,128)}) fusion(pred[512,512]{0,1:T(8,128)(4,1)S(1)} %and_or_fusion.2, bf16[512,2,4,80]{0,3,2,1:T(8,128)(2,1)} %bitcast.189, bf16[512,2,80]{0,2,1:T(8,128)(2,1)} %get-tuple-element.391), kind=kOutput, calls=%fused_computation.7.clone.1 | convolution fusion | flops 341831680 | bytes 9486336 | tf_op jit(solution)/shard_map/while/body/eval_jaxpr/nkgd,mkd->nkgm/dot_general | solution.py:34
  120.1 4.6 %fusion.85 = f32[512,2,4]{0,2,1:T(4,128)S(1)} fusion(f32[2,512,4,512]{1,3,2,0:T(8,128)} %get-tuple-element.359, f32[512,2,4]{0,2,1:T(4,128)S(1)} %get-tuple-element.358, pred[512,512]{0,1:T(8,128)(4,1)S(1)} %and_or_fusion.2), kind=kLoop, calls=%fused_computation.12.clone.1 | loop fusion | flops 10481664 | bytes 8683520 | tf_op jit(solution)/shard_map/while/body/eval_jaxpr/reduce_sum | solution.py:41
  126.0 2.3 fusion.86
  128.3 2.4 copy.197
  130.8 24.2 %dynamic_update_slice.19 = f32[2,512,2,4,80]{1,0,4,3,2:T(2,128)} dynamic-update-slice(f32[2,512,2,4,80]{1,0,4,3,2:T(2,128)} %get-tuple-element.375, f32[1,512,2,4,80]{1,0,4,3,2:T(1,128)} %copy.197, s32[]{:T(128)S(6)} %copy.205, s32[]{:T(128)} %constant.138.clone.1..sunk, s32[]{:T(128)} %constant.138.clone.1..sunk, s32[]{:T(128)} %constant.138.clone.1..sunk, s32[]{:T(128)} %constant.138.clone.1..sunk) | dynamic-update-slice | bytes 2621444 | tf_op jit(solution)/shard_map/while/body/jit(dynamic_update_index_in_dim)/dynamic_update_slice | solution.py:126
  156.5 4.0 all-to-all-start.1
  162.1 1.8 gather_fusion
  165.4 4.1 all-to-all-start.2
  169.5 2.0 pad_maximum_fusion
  171.4 1.9 gather_fusion.1
  173.4 2.3 reshape.447
  175.7 3.7 reshape.446
  179.4 4.7 %reshape.442 = f32[8,128,2,4,80]{1,0,4,3,2:T(8,128)} reshape(f32[2,512,2,4,80]{1,0,4,3,2:T(2,128)} %get-tuple-element.70) | data formatting | bytes 5242880 | tf_op jit(solution)/shard_map/reshape | solution.py:136
  184.1 3.7 copy.133
  188.5 4.4 %all-to-all-start = ((f32[8,128,2,4,80]{1,4,3,2,0:T(8,128)}), f32[8,128,2,4,80]{1,4,3,2,0:T(8,128)}, u32[]{:S(2)}, u32[]{:S(2)}) async-start(f32[8,128,2,4,80]{1,4,3,2,0:T(8,128)} %copy.133), calls=%async_computation | async-start | bytes 5242880 | tf_op jit(solution)/shard_map/all_to_all | solution.py:141
  193.2 3.7 fusion.61
  199.3 1.9 convolution_bitcast_fusion
  203.0 2.9 gather_fusion.3
  205.9 2.0 copy.148
  209.7 2.5 fusion.30
  217.3 7.9 %all-to-all-done = f32[8,128,2,4,80]{1,4,3,2,0:T(8,128)} async-done(((f32[8,128,2,4,80]{1,4,3,2,0:T(8,128)}), f32[8,128,2,4,80]{1,4,3,2,0:T(8,128)}, u32[]{:S(2)}, u32[]{:S(2)}) %all-to-all-start) | async-done | bytes 2621472 | tf_op jit(solution)/shard_map/all_to_all | solution.py:141
  225.2 2.1 multiply_reduce_fusion
  227.4 1.8 fusion.66
  229.5 97.3 %all-gather.6.cloned.1.call-done = f32[512,2560]{1,0:T(8,128)} async-done(((f32[128,2560]{1,0:T(8,128)}), f32[512,2560]{1,0:T(8,128)}) %all-gather.6.cloned.1.call-update) | async-done | bytes 5242896 | tf_op jit(solution)/shard_map/all_gather | solution.py:197
  326.8 4.1 reduce_sum.129
  330.9 1.8 fusion.24
  333.5 4.0 fusion.45
  337.5 6.7 %fusion.29 = f32[128,2560]{1,0:T(8,128)} fusion(bf16[896,2560]{1,0:T(8,128)(2,1)} %param.40, bf16[2560,896]{1,0:T(8,128)(2,1)} %param.39, f32[128,896]{1,0:T(8,128)} %fusion.45, bf16[128,2560]{1,0:T(8,128)(2,1)} %copy-done.3, f32[2560]{0:T(1024)S(1)} %convert_element_type.63, f32[128]{0:T(128)S(1)} %add_rsqrt_fusion.1), kind=kOutput, calls=%fused_computation.50 | convolution fusion | flops 1176403968 | bytes 11610624 | tf_op jit(solution)/shard_map/dot_general | solution.py:207
  345.1 57.7 %all-reduce.2.cloned.1.call-done = f32[128,2560]{1,0:T(8,128)} async-done(((f32[128,2560]{1,0:T(8,128)}), f32[128,2560]{1,0:T(8,128)}) %all-reduce.2.cloned.1.call-update) | async-done | bytes 1310736 | tf_op jit(solution)/shard_map/psum | solution.py:207
  402.8 1.9 fusion.21
  404.7 2.7 convolution_convert_fusion.1
  (137 shorter events, 40.5 us)
Async XLA Ops:
  7.2 220.2 %copy-start = (bf16[640,2560]{1,0:T(8,128)(2,1)S(1)}, bf16[640,2560]{1,0:T(8,128)(2,1)}, u32[]{:S(2)}) copy-start(bf16[640,2560]{1,0:T(8,128)(2,1)} %param.36) | copy-start | bytes 9830404
  7.2 26.5 %copy-start.11 = (s32[4,128]{1,0:T(4,128)S(1)}, s32[4,128]{1,0:T(4,128)}, u32[]{:S(2)}) copy-start(s32[4,128]{1,0:T(4,128)} %constant.143.clone.1) | copy-start | bytes 6148
  7.2 12.8 %copy-start.14 = (s32[16]{0:T(128)S(1)}, s32[16]{0:T(128)}, u32[]{:S(2)}) copy-start(s32[16]{0:T(128)} %param.30) | copy-start | bytes 196
  7.2 13.4 %copy-start.19 = (s32[6]{0:T(128)S(1)}, s32[6]{0:T(128)}, u32[]{:S(2)}) copy-start(s32[6]{0:T(128)} %param.31) | copy-start | bytes 76
  7.2 13.5 %copy-start.15 = (s32[8]{0:T(128)S(1)}, s32[8]{0:T(128)}, u32[]{:S(2)}) copy-start(s32[8]{0:T(128)} %param.32) | copy-start | bytes 100
  7.2 25.0 %copy-start.5 = (s32[32]{0:T(128)S(1)}, s32[32]{0:T(128)}, u32[]{:S(2)}) copy-start(s32[32]{0:T(128)} %param.34) | copy-start | bytes 388
  7.2 30.9 %copy-start.20 = (s32[32]{0:T(128)S(1)}, s32[32]{0:T(128)}, u32[]{:S(2)}) copy-start(s32[32]{0:T(128)} %param.35) | copy-start | bytes 388
  7.2 47.4 %all-gather.4.cloned.1.call-start = ((), (), s32[]{:S(2)}) async-start(), calls=%async_computation.3 | async-start | bytes 1474560 | tf_op jit(solution)/shard_map/all_gather | solution.py:114
  15.7 5.0 %copy-start.21 = (s32[128]{0:T(128)}, s32[128]{0:T(128)S(1)}, u32[]{:S(2)}) copy-start(s32[128]{0:T(128)S(1)} %convert_reduce_fusion) | copy-start | bytes 1540
  69.9 5.8 %copy-start.1 = (f32[2,512,4,512]{1,3,2,0:T(8,128)S(1)}, f32[2,512,4,512]{1,3,2,0:T(8,128)}, u32[]{:S(2)}) copy-start(f32[2,512,4,512]{1,3,2,0:T(8,128)} %get-tuple-element.359) | copy-start | bytes 25165828 | tf_op jit(solution)/shard_map/while
  69.9 5.8 %copy-start.7 = (bf16[512,2,80]{0,2,1:T(8,128)(2,1)S(1)}, bf16[512,2,80]{0,2,1:T(8,128)(2,1)}, u32[]{:S(2)}) copy-start(bf16[512,2,80]{0,2,1:T(8,128)(2,1)} %get-tuple-element.392) | copy-start | bytes 491524 | tf_op jit(solution)/shard_map/while
  78.1 2.4 copy-start.9
  80.6 24.2 %copy-start.10 = (f32[2,512,2,4]{1,0,3,2:T(2,128)}, f32[2,512,2,4]{1,0,3,2:T(2,128)S(1)}, u32[]{:S(2)}) copy-start(f32[2,512,2,4]{1,0,3,2:T(2,128)S(1)} %dynamic_update_slice.18) | copy-start | bytes 98308 | tf_op jit(solution)/shard_map/while
  120.1 5.8 %copy-start.1 = (f32[2,512,4,512]{1,3,2,0:T(8,128)S(1)}, f32[2,512,4,512]{1,3,2,0:T(8,128)}, u32[]{:S(2)}) copy-start(f32[2,512,4,512]{1,3,2,0:T(8,128)} %get-tuple-element.359) | copy-start | bytes 25165828 | tf_op jit(solution)/shard_map/while
  120.1 5.8 %copy-start.7 = (bf16[512,2,80]{0,2,1:T(8,128)(2,1)S(1)}, bf16[512,2,80]{0,2,1:T(8,128)(2,1)}, u32[]{:S(2)}) copy-start(bf16[512,2,80]{0,2,1:T(8,128)(2,1)} %get-tuple-element.392) | copy-start | bytes 491524 | tf_op jit(solution)/shard_map/while
  128.3 2.4 copy-start.9
  130.8 24.2 %copy-start.10 = (f32[2,512,2,4]{1,0,3,2:T(2,128)}, f32[2,512,2,4]{1,0,3,2:T(2,128)S(1)}, u32[]{:S(2)}) copy-start(f32[2,512,2,4]{1,0,3,2:T(2,128)S(1)} %dynamic_update_slice.18) | copy-start | bytes 98308 | tf_op jit(solution)/shard_map/while
  155.1 16.4 %copy-start.2 = (bf16[128,640]{1,0:T(8,128)(2,1)S(1)}, bf16[128,640]{1,0:T(8,128)(2,1)}, u32[]{:S(2)}) copy-start(bf16[128,640]{1,0:T(8,128)(2,1)} %param.24) | copy-start | bytes 491524
  156.5 8.8 %all-to-all-start.1 = ((f32[8,128,2,4]{1,3,2,0:T(4,128)}), f32[8,128,2,4]{1,3,2,0:T(4,128)}, u32[]{:S(2)}, u32[]{:S(2)}) async-start(f32[8,128,2,4]{1,3,2,0:T(4,128)} %copy.135), calls=%async_computation.1 | async-start | bytes 65536 | tf_op jit(solution)/shard_map/all_to_all | solution.py:139
  165.4 22.5 %all-to-all-start.2 = ((f32[8,128,2,4]{1,3,2,0:T(4,128)}), f32[8,128,2,4]{1,3,2,0:T(4,128)S(1)}, u32[]{:S(2)}, u32[]{:S(2)}) async-start(f32[8,128,2,4]{1,3,2,0:T(4,128)} %copy.150), calls=%async_computation.2 | async-start | bytes 65536 | tf_op jit(solution)/shard_map/all_to_all | solution.py:140
  187.9 5.1 %copy-start.16 = (s32[16]{0:T(128)S(1)}, s32[16]{0:T(128)}, u32[]{:S(2)}) copy-start(s32[16]{0:T(128)} %param.28) | copy-start | bytes 196
  187.9 0.6 copy-start.8
  188.5 36.7 %all-to-all-start = ((f32[8,128,2,4,80]{1,4,3,2,0:T(8,128)}), f32[8,128,2,4,80]{1,4,3,2,0:T(8,128)}, u32[]{:S(2)}, u32[]{:S(2)}) async-start(f32[8,128,2,4,80]{1,4,3,2,0:T(8,128)} %copy.133), calls=%async_computation | async-start | bytes 5242880 | tf_op jit(solution)/shard_map/all_to_all | solution.py:141
  192.9 133.9 %all-gather.6.cloned.1.call-start = ((), (), s32[]{:S(2)}) async-start(), calls=%async_computation.5 | async-start | bytes 6553600 | tf_op jit(solution)/shard_map/all_gather | solution.py:197
  193.0 4.0 copy-start.6
  201.2 1.8 copy-start.17
  201.2 1.8 copy-start.22
  225.2 2.1 copy-start.4
  227.3 2.1 copy-start.12
  229.2 173.6 %all-reduce.2.cloned.1.call-start = ((), (), s32[]{:S(2)}) async-start(), calls=%async_computation.4 | async-start | bytes 2621440 | tf_op jit(solution)/shard_map/psum | solution.py:207
  332.6 0.9 copy-start.3
  337.5 6.8 %copy-start.13 = (bf16[2560]{0:T(1024)(128)(2,1)S(1)}, bf16[2560]{0:T(1024)(128)(2,1)}, u32[]{:S(2)}) copy-start(bf16[2560]{0:T(1024)(128)(2,1)} %param.41) | copy-start | bytes 15364
  402.8 4.7 %copy-start.18 = (bf16[2560,640]{1,0:T(8,128)(2,1)S(1)}, bf16[2560,640]{1,0:T(8,128)(2,1)}, u32[]{:S(2)}) copy-start(bf16[2560,640]{1,0:T(8,128)(2,1)} %param.42) | copy-start | bytes 9830404
Sparse Core Ops, SparseCore 0:
  10.0 27.2 all-gather.3
  229.3 97.4 all-gather.5
  344.4 58.3 all-reduce.1
